TPU v7x, 32 devices: a whole 2x2x4 slice. The times are simulated.
32 devices in a mesh: row: 4 (over y, core), col: 8 (over z, x).
Axes of the slice: x: 2, y: 2, z: 4, core: 2. Of those that a mesh axis runs over, the one named last changes fastest.
Arguments:
- inputs: bfloat16 [512, 12288], P('col', 'row'), may hold values from -6 to 6
- grad_out: bfloat16 [512, 12288], P('col', 'row'), may hold values from -6 to 6
- w_in: bfloat16 [12288, 24576], P('row', 'col'), may hold values from -0.0546875 to 0.0546875
- w_out: bfloat16 [24576, 12288], P('col', 'row'), may hold values from -0.0390625 to 0.0390625
Outputs:
- outputs: bfloat16 [512, 12288], P('col', 'row')
- grad_in: bfloat16 [512, 12288], P('col', 'row')
- grad_w_in: bfloat16 [12288, 24576], P('row', 'col')
- grad_w_out: bfloat16 [24576, 12288], P('col', 'row')
All inputs are finite; a program needn't handle non-finite values.
Results may differ from a plain program's by a relative error of at most 0.019.
Values may be sent and summed in bfloat16 or wider, within the bound.
A program may use at most 192 MiB of HBM per device.

v0:
```python
from functools import partial
import jax
import jax.numpy as jnp
from jax import lax
from jax.sharding import PartitionSpec as P


def col_panel(values):
    return lax.all_gather(values, "col", axis=0, tiled=True)


def contract(left, right, dims):
    return lax.dot_general(
        left, right, ((dims[0], dims[1]), ((), ())), preferred_element_type=jnp.float32
    )


def row_sums(left, right, dims):
    return lax.psum_scatter(
        contract(left, right, dims).astype(jnp.bfloat16), "row", scatter_dimension=0, tiled=True
    ).astype(jnp.float32)


def row_spread(values):
    return lax.all_gather(values, "row", axis=0, tiled=True)


def col_sums(left, right, dims):
    return lax.psum_scatter(
        contract(
            lax.dynamic_slice_in_dim(
                left, jnp.int32(0), left.shape[0] // lax.axis_size("col") * lax.axis_size("col"), 0
            ),
            right,
            dims,
        ).astype(jnp.bfloat16),
        "col",
        scatter_dimension=0,
        tiled=True,
    ).astype(jnp.float32)


def local(inputs, grad_out, w_in, w_out):
    gelu_tanh = partial(jax.nn.gelu, approximate=True)
    input_all = col_panel(inputs)
    cotan_all = None
    hidden_pre = row_sums(input_all, w_in, ((1,), (0,)))
    act_all = row_spread(gelu_tanh(hidden_pre).astype(jnp.bfloat16))
    outputs = col_sums(act_all, w_out, ((1,), (0,))).astype(jnp.bfloat16)
    cotan_all = col_panel(grad_out)
    grad_act = row_sums(cotan_all, w_out, ((1,), (1,)))
    grad_pre = jax.vjp(gelu_tanh, hidden_pre)[1](grad_act)[0].astype(jnp.bfloat16)
    grad_pre_all = row_spread(grad_pre)
    grad_w_out = contract(act_all, cotan_all, ((0,), (0,))).astype(jnp.bfloat16)
    grad_w_in = contract(input_all, grad_pre_all, ((0,), (0,))).astype(jnp.bfloat16)
    grad_in = col_sums(grad_pre_all, w_in, ((1,), (1,))).astype(jnp.bfloat16)
    return (outputs, grad_in, grad_w_in, grad_w_out)


def solution(mesh):
    placed = (P("col", "row"), P("col", "row"), P("row", "col"), P("col", "row"))
    return jax.shard_map(
        local,
        mesh=mesh,
        in_specs=placed,
        out_specs=(P("col", "row"), P("col", "row"), P("row", "col"), P("col", "row")),
        check_vma=False,
    )
```

profile of v0, /device:TPU:0, one launch (start us, length us, event | category | flops | bytes accessed | tf_op | source)
XLA Modules:
  0.0 441.4 jit_solution(10468758725500619523)
XLA Ops:
  7.2 0.0 all-gather.9.cloned.1.call-start
  7.2 0.7 all-gather.9.cloned.1.call-update
  7.9 0.0 all-gather.5.cloned.1.call-start
  7.9 0.7 all-gather.5.cloned.1.call-update
  8.6 0.0 reduce-scatter.9.cloned.1.call-start
  8.7 64.7 %all-gather.9.cloned.1.call-done = bf16[512,3072]{1,0:T(8,128)(2,1)} async-done(((bf16[64,3072]{1,0:T(8,128)(2,1)}), bf16[512,3072]{1,0:T(8,128)(2,1)}) %all-gather.9.cloned.1.call-update) | async-done | bytes 3145744 | tf_op jit(solution)/shard_map/all_gather | solution.py:9
  73.4 15.9 %convolution_convert_fusion.2 = bf16[512,3072]{1,0:T(8,128)(2,1)} fusion(bf16[512,3072]{1,0:T(8,128)(2,1)} %all-gather.9.cloned.1.call-done, bf16[3072,3072]{1,0:T(8,128)(2,1)} %param.7), kind=kOutput, calls=%fused_computation.3 | convolution fusion | flops 9665249280 | bytes 25165824 | tf_op jit(solution)/shard_map/dot_general | solution.py:13
  89.2 0.0 reduce-scatter.9.cloned.1.call-update
  89.3 0.0 reduce-scatter.5.cloned.1.call-start
  89.3 45.4 %all-gather.5.cloned.1.call-done = bf16[512,3072]{1,0:T(8,128)(2,1)} async-done(((bf16[64,3072]{1,0:T(8,128)(2,1)}), bf16[512,3072]{1,0:T(8,128)(2,1)}) %all-gather.5.cloned.1.call-update) | async-done | bytes 3145744 | tf_op jit(solution)/shard_map/all_gather | solution.py:9
  134.7 15.8 %convolution_convert_fusion.4 = bf16[512,3072]{1,0:T(8,128)(2,1)} fusion(bf16[512,3072]{1,0:T(8,128)(2,1)} %all-gather.5.cloned.1.call-done, bf16[3072,3072]{1,0:T(8,128)(2,1)} %param.6), kind=kOutput, calls=%fused_computation.5 | convolution fusion | flops 9665249280 | bytes 25165824 | tf_op jit(solution)/shard_map/dot_general | solution.py:13
  150.4 0.0 reduce-scatter.5.cloned.1.call-update
  150.5 0.0 all-gather.7.cloned.1.call-start
  150.5 23.9 %reduce-scatter.9.cloned.1.call-done = bf16[128,3072]{1,0:T(8,128)(2,1)} async-done(((bf16[512,3072]{1,0:T(8,128)(2,1)}), bf16[128,3072]{1,0:T(8,128)(2,1)}) %reduce-scatter.9.cloned.1.call-update) | async-done | bytes 786448 | tf_op jit(solution)/shard_map/reduce_scatter | solution.py:19
  174.4 41.1 %reduce-scatter.5.cloned.1.call-done = bf16[128,3072]{1,0:T(8,128)(2,1)} async-done(((bf16[512,3072]{1,0:T(8,128)(2,1)}), bf16[128,3072]{1,0:T(8,128)(2,1)}) %reduce-scatter.5.cloned.1.call-update) | async-done | bytes 786448 | tf_op jit(solution)/shard_map/reduce_scatter | solution.py:19
  215.5 3.7 fusion.3
  219.2 0.0 all-gather.7.cloned.1.call-update
  219.3 0.0 all-gather.11.cloned.1.call-start
  219.3 0.5 all-gather.11.cloned.1.call-update
  219.8 0.0 reduce-scatter.7.cloned.1.call-start
  219.9 28.1 %all-gather.7.cloned.1.call-done = bf16[512,3072]{1,0:T(8,128)(2,1)} async-done(((bf16[128,3072]{1,0:T(8,128)(2,1)}), bf16[512,3072]{1,0:T(8,128)(2,1)}) %all-gather.7.cloned.1.call-update) | async-done | bytes 3145744 | tf_op jit(solution)/shard_map/all_gather | solution.py:25
  248.0 15.8 %convolution_convert_fusion.3 = bf16[512,3072]{1,0:T(8,128)(2,1)} fusion(bf16[512,3072]{1,0:T(8,128)(2,1)} %all-gather.7.cloned.1.call-done, bf16[3072,3072]{1,0:T(8,128)(2,1)} %param.7), kind=kOutput, calls=%fused_computation.4 | convolution fusion | flops 9665249280 | bytes 25165824 | tf_op jit(solution)/shard_map/dot_general | solution.py:13
  263.8 0.0 reduce-scatter.7.cloned.1.call-update
  263.8 0.2 reduce-scatter.11.cloned.1.call-start
  264.0 14.5 %all-gather.11.cloned.1.call-done = bf16[512,3072]{1,0:T(8,128)(2,1)} async-done(((bf16[128,3072]{1,0:T(8,128)(2,1)}), bf16[512,3072]{1,0:T(8,128)(2,1)}) %all-gather.11.cloned.1.call-update) | async-done | bytes 3145744 | tf_op jit(solution)/shard_map/all_gather | solution.py:25
  278.5 15.9 %convolution_convert_fusion.1 = bf16[512,3072]{1,0:T(8,128)(2,1)} fusion(bf16[512,3072]{1,0:T(8,128)(2,1)} %all-gather.11.cloned.1.call-done, bf16[3072,3072]{1,0:T(8,128)(2,1)} %param.6), kind=kOutput, calls=%fused_computation.2 | convolution fusion | flops 9665249280 | bytes 25165824 | tf_op jit(solution)/shard_map/dot_general | solution.py:13
  294.5 1.9 copy-done.1
  296.4 15.1 %convert_bitcast_fusion = bf16[3072,3072]{0,1:T(8,128)(2,1)} fusion(bf16[512,3072]{1,0:T(8,128)(2,1)} %all-gather.11.cloned.1.call-done, bf16[512,3072]{1,0:T(8,128)(2,1)S(1)} %copy-done.1), kind=kOutput, calls=%fused_computation | convolution fusion | flops 9673113600 | bytes 25165824 | tf_op jit(solution)/shard_map/dot_general | solution.py:13
  311.5 24.8 %copy.8 = bf16[3072,3072]{1,0:T(8,128)(2,1)} copy(bf16[3072,3072]{0,1:T(8,128)(2,1)} %convert_bitcast_fusion) | data formatting | bytes 37748736
  336.3 15.0 %convolution_convert_fusion = bf16[3072,3072]{1,0:T(8,128)(2,1)} fusion(bf16[512,3072]{1,0:T(8,128)(2,1)} %all-gather.7.cloned.1.call-done, bf16[512,3072]{1,0:T(8,128)(2,1)S(1)} %copy-done), kind=kOutput, calls=%fused_computation.1 | convolution fusion | flops 9673113600 | bytes 25165824 | tf_op jit(solution)/shard_map/dot_general | solution.py:13
  351.3 5.6 %reduce-scatter.7.cloned.1.call-done = bf16[64,3072]{1,0:T(8,128)(2,1)} async-done(((bf16[512,3072]{1,0:T(8,128)(2,1)}), bf16[64,3072]{1,0:T(8,128)(2,1)}) %reduce-scatter.7.cloned.1.call-update) | async-done | bytes 393232 | tf_op jit(solution)/shard_map/reduce_scatter | solution.py:29
  356.9 77.6 %reduce-scatter.11.cloned.1.call-done = bf16[64,3072]{1,0:T(8,128)(2,1)} async-done(((bf16[512,3072]{1,0:T(8,128)(2,1)}), bf16[64,3072]{1,0:T(8,128)(2,1)}) %reduce-scatter.11.cloned.1.call-update) | async-done | bytes 393232 | tf_op jit(solution)/shard_map/reduce_scatter | solution.py:29
  (4 shorter events, 0.0 us)
Async XLA Ops:
  7.2 66.2 %all-gather.9.cloned.1.call-start = ((), (), s32[]{:S(2)}) async-start(), calls=%async_computation.8 | async-start | bytes 3538944 | tf_op jit(solution)/shard_map/all_gather | solution.py:9
  7.9 126.8 %all-gather.5.cloned.1.call-start = ((), (), s32[]{:S(2)}) async-start(), calls=%async_computation.4 | async-start | bytes 3538944 | tf_op jit(solution)/shard_map/all_gather | solution.py:9
  8.6 165.7 %reduce-scatter.9.cloned.1.call-start = ((), (), s32[]{:S(2)}) async-start(), calls=%async_computation.9 | async-start | bytes 3932160 | tf_op jit(solution)/shard_map/reduce_scatter | solution.py:19
  89.3 126.2 %reduce-scatter.5.cloned.1.call-start = ((), (), s32[]{:S(2)}) async-start(), calls=%async_computation.5 | async-start | bytes 3932160 | tf_op jit(solution)/shard_map/reduce_scatter | solution.py:19
  150.5 97.5 %all-gather.7.cloned.1.call-start = ((), (), s32[]{:S(2)}) async-start(), calls=%async_computation.6 | async-start | bytes 3932160 | tf_op jit(solution)/shard_map/all_gather | solution.py:25
  219.3 59.3 %all-gather.11.cloned.1.call-start = ((), (), s32[]{:S(2)}) async-start(), calls=%async_computation.10 | async-start | bytes 3932160 | tf_op jit(solution)/shard_map/all_gather | solution.py:25
  219.8 137.1 %reduce-scatter.7.cloned.1.call-start = ((), (), s32[]{:S(2)}) async-start(), calls=%async_computation.7 | async-start | bytes 3538944 | tf_op jit(solution)/shard_map/reduce_scatter | solution.py:29
  263.8 170.7 %reduce-scatter.11.cloned.1.call-start = ((), (), s32[]{:S(2)}) async-start(), calls=%async_computation.11 | async-start | bytes 3538944 | tf_op jit(solution)/shard_map/reduce_scatter | solution.py:29
  294.5 1.9 copy-start.1
  311.5 24.8 %copy-start = (bf16[512,3072]{1,0:T(8,128)(2,1)S(1)}, bf16[512,3072]{1,0:T(8,128)(2,1)}, u32[]{:S(2)}) copy-start(bf16[512,3072]{1,0:T(8,128)(2,1)} %all-gather.9.cloned.1.call-done) | copy-start | bytes 9437188
Sparse Core Ops, SparseCore 0:
  10.2 63.1 all-gather.8
  75.5 59.0 all-gather.4
  137.8 36.5 reduce-scatter.8
  177.5 37.9 reduce-scatter.4
  219.4 28.5 all-gather.6
  249.9 28.5 all-gather.10
  282.7 74.2 reduce-scatter.6
  361.1 73.3 reduce-scatter.10
where the time goes:
time: 442 us; the launch traced here: 441 us
  waiting for transfers between devices  303 us (69%)
  matrix products  93.5 us (21%)
  local copies, waits for them, and re-layouts  26.7 us (6%)
  between operations  14.1 us (3%)
    all_gather x2, waiting for transfers between devices, col_panel(): return lax.all_gather(values, 'col', axis=0, tiled=True)  110 us
    dot_general x6, matrix products, contract(): lax.dot_general(left, right, ((dims[0], dims[1]), ((), ())), preferred_el...  93.5 us
    reduce_scatter x2, waiting for transfers between devices, col_sums(): lax.psum_scatter(contract(lax.dynamic_slice_in_dim(left, jnp.int32(0), le...  83.2 us
    reduce_scatter x2, waiting for transfers between devices, row_sums(): lax.psum_scatter(contract(left, right, dims).astype(jnp.bfloat16), 'row',...  65 us
    all_gather x2, waiting for transfers between devices, row_spread(): return lax.all_gather(values, 'row', axis=0, tiled=True)  42.5 us
    unnamed x5, local copies, waits for them, and re-layouts  26.7 us
  transfers between devices with their start and end apart: 8, of which 8 were waited for; matrix products, arithmetic and copies ran while one was open for 27% of the time, Pallas kernels for 0%

commit v1 on v0

--- a/solution.py
+++ b/solution.py
@@ -3,6 +3,19 @@
 import jax.numpy as jnp
 from jax import lax
 from jax.sharding import PartitionSpec as P
+
+
+def see_runs_on_mesh(x0, chip_axis):
+    block_out, before, r1 = (lax.axis_size(chip_axis), lax.axis_index(chip_axis), x0.shape[0])
+    store = list(map(lambda ii: (ii, (ii + 1) % block_out), range(block_out)))
+    n_now = jnp.zeros((*x0.shape[:0], block_out * r1, *x0.shape[1:]), x0.dtype)
+    p_next = x0
+    for i0 in range(block_out):
+        answer = (before - i0) % block_out
+        n_now = lax.dynamic_update_slice_in_dim(n_now, p_next, answer * r1, axis=0)
+        if i0 < block_out - 1:
+            p_next = lax.ppermute(p_next, axis_name=chip_axis, perm=store)
+    return n_now
 
 
 def col_panel(values):
@@ -22,7 +35,7 @@
 
 
 def row_spread(values):
-    return lax.all_gather(values, "row", axis=0, tiled=True)
+    return see_runs_on_mesh(values, "row")
 
 
 def col_sums(left, right, dims):

time: 442 us -> 412 us (0.932)
  waiting for transfers between devices: 303 us -> 265 us
  local copies, waits for them, and re-layouts: 26.7 us -> 31.8 us
  starting transfers between devices: 0.5 us -> 4.93 us
    ppermute x0 -> x6, waiting for transfers between devices: none -> 59.6 us  [see_runs_on_mesh(): p_next = lax.ppermute(p_next, axis_name=chip_axis, perm=store)]
    all_gather x2 -> x0, waiting for transfers between devices: 42.5 us -> none  [row_spread(): return lax.all_gather(values, 'row', axis=0, tiled=True)]
    reduce_scatter x2, waiting for transfers between devices: 83.2 us -> 41.5 us  [col_sums(): lax.psum_scatter(contract(lax.dynamic_slice_in_dim(left, jnp.int32(0), le...]
    reduce_scatter x2, waiting for transfers between devices: 65 us -> 35.9 us  [row_sums(): lax.psum_scatter(contract(left, right, dims).astype(jnp.bfloat16), 'row',...]
    all_gather x2, waiting for transfers between devices: 110 us -> 127 us  [col_panel(): return lax.all_gather(values, 'col', axis=0, tiled=True)]
    ppermute x0 -> x6, starting transfers between devices: none -> 4.7 us  [see_runs_on_mesh(): p_next = lax.ppermute(p_next, axis_name=chip_axis, perm=store)]
    unnamed x5 -> x13, local copies, waits for them, and re-layouts: 26.7 us -> 30.7 us
  transfers between devices with their start and end apart: 8 -> 12, of which waited for: 8 -> 9; matrix products, arithmetic and copies ran while one was open for 27% -> 26% of each run, Pallas kernels for 0% -> 0%
where the time goes in v1:
time: 412 us
  waiting for transfers between devices  265 us (64%)
  matrix products  91.9 us (22%)
  local copies, waits for them, and re-layouts  31.8 us (8%)
  between operations  14.3 us (3%)
  starting transfers between devices  4.93 us (1%)
    all_gather x2, waiting for transfers between devices, col_panel(): return lax.all_gather(values, 'col', axis=0, tiled=True)  127 us
    dot_general x6, matrix products, contract(): lax.dot_general(left, right, ((dims[0], dims[1]), ((), ())), preferred_el...  91.9 us
    ppermute x6, waiting for transfers between devices, see_runs_on_mesh(): p_next = lax.ppermute(p_next, axis_name=chip_axis, perm=store)  59.6 us
    reduce_scatter x2, waiting for transfers between devices, col_sums(): lax.psum_scatter(contract(lax.dynamic_slice_in_dim(left, jnp.int32(0), le...  41.5 us
    reduce_scatter x2, waiting for transfers between devices, row_sums(): lax.psum_scatter(contract(left, right, dims).astype(jnp.bfloat16), 'row',...  35.9 us
    unnamed x13, local copies, waits for them, and re-layouts  30.7 us
  transfers between devices with their start and end apart: 12, of which 9 were waited for; matrix products, arithmetic and copies ran while one was open for 26% of the time, Pallas kernels for 0%

profile of v1, /device:TPU:0, one launch (start us, length us, event | category | flops | bytes accessed | tf_op | source)
XLA Modules:
  0.0 411.6 jit_solution(5870611346100683949)
XLA Ops:
  7.2 0.7 all-gather.3.cloned.1.call-update
  7.9 65.4 %all-gather.3.cloned.1.call-done = bf16[512,3072]{1,0:T(8,128)(2,1)} async-done(((bf16[64,3072]{1,0:T(8,128)(2,1)}), bf16[512,3072]{1,0:T(8,128)(2,1)}) %all-gather.3.cloned.1.call-update) | async-done | bytes 3145744 | tf_op jit(solution)/shard_map/all_gather | solution.py:22
  73.4 15.9 %convolution_convert_fusion.4 = bf16[512,3072]{1,0:T(8,128)(2,1)} fusion(bf16[512,3072]{1,0:T(8,128)(2,1)} %all-gather.3.cloned.1.call-done, bf16[3072,3072]{1,0:T(8,128)(2,1)} %param.6), kind=kOutput, calls=%fused_computation.5 | convolution fusion | flops 9665249280 | bytes 25165824 | tf_op jit(solution)/shard_map/dot_general | solution.py:26
  89.3 0.7 all-gather.5.cloned.1.call-update
  90.0 35.9 %reduce-scatter.5.cloned.1.call-done = bf16[128,3072]{1,0:T(8,128)(2,1)} async-done(((bf16[512,3072]{1,0:T(8,128)(2,1)}), bf16[128,3072]{1,0:T(8,128)(2,1)}) %reduce-scatter.5.cloned.1.call-update) | async-done | bytes 786448 | tf_op jit(solution)/shard_map/reduce_scatter | solution.py:32
  126.0 1.7 fusion.8
  127.7 61.2 %all-gather.5.cloned.1.call-done = bf16[512,3072]{1,0:T(8,128)(2,1)} async-done(((bf16[64,3072]{1,0:T(8,128)(2,1)}), bf16[512,3072]{1,0:T(8,128)(2,1)}) %all-gather.5.cloned.1.call-update) | async-done | bytes 3145744 | tf_op jit(solution)/shard_map/all_gather | solution.py:22
  188.9 15.9 %convolution_convert_fusion.2 = bf16[512,3072]{1,0:T(8,128)(2,1)} fusion(bf16[512,3072]{1,0:T(8,128)(2,1)} %all-gather.5.cloned.1.call-done, bf16[3072,3072]{1,0:T(8,128)(2,1)} %param.7), kind=kOutput, calls=%fused_computation.3 | convolution fusion | flops 9665249280 | bytes 25165824 | tf_op jit(solution)/shard_map/dot_general | solution.py:26
  205.0 11.3 %collective-permute-done.1 = bf16[128,3072]{1,0:T(8,128)(2,1)S(1)} collective-permute-done((bf16[128,3072]{1,0:T(8,128)(2,1)S(1)}, bf16[128,3072]{1,0:T(8,128)(2,1)S(1)}, u32[]{:S(2)}, u32[]{:S(2)}) %collective-permute-start.1) | collective-permute-done | bytes 786464 | tf_op jit(solution)/shard_map/ppermute | solution.py:17
  216.3 0.4 broadcast.20.clone
  216.7 0.6 constant_dynamic-update-slice_fusion.7
  217.3 0.1 constant_dynamic-update-slice_fusion.6
  217.4 18.7 %collective-permute-done.2 = bf16[128,3072]{1,0:T(8,128)(2,1)S(1)} collective-permute-done((bf16[128,3072]{1,0:T(8,128)(2,1)S(1)}, bf16[128,3072]{1,0:T(8,128)(2,1)S(1)}, u32[]{:S(2)}, u32[]{:S(2)}) %collective-permute-start.2) | collective-permute-done | bytes 786464 | tf_op jit(solution)/shard_map/ppermute | solution.py:17
  236.3 1.6 copy-done.3
  237.9 15.0 %convolution_convert_fusion.3 = bf16[512,3072]{1,0:T(8,128)(2,1)} fusion(bf16[512,3072]{1,0:T(8,128)(2,1)S(1)} %constant_dynamic-update-slice_fusion.4, bf16[3072,3072]{1,0:T(8,128)(2,1)} %param.7), kind=kOutput, calls=%fused_computation.4 | convolution fusion | flops 9665249280 | bytes 25165824 | tf_op jit(solution)/shard_map/dot_general | solution.py:26
  253.1 0.4 broadcast.20.clone.1
  253.4 0.7 copy-done.5
  254.2 1.2 constant_dynamic-update-slice_fusion.3
  255.4 1.6 collective-permute-start.3
  256.9 9.9 %collective-permute-done.3 = bf16[128,3072]{1,0:T(8,128)(2,1)S(1)} collective-permute-done((bf16[128,3072]{1,0:T(8,128)(2,1)S(1)}, bf16[128,3072]{1,0:T(8,128)(2,1)S(1)}, u32[]{:S(2)}, u32[]{:S(2)}) %collective-permute-start.3) | collective-permute-done | bytes 786464 | tf_op jit(solution)/shard_map/ppermute | solution.py:17
  266.8 1.5 collective-permute-start.4
  268.3 9.9 %collective-permute-done.4 = bf16[128,3072]{1,0:T(8,128)(2,1)S(1)} collective-permute-done((bf16[128,3072]{1,0:T(8,128)(2,1)S(1)}, bf16[128,3072]{1,0:T(8,128)(2,1)S(1)}, u32[]{:S(2)}, u32[]{:S(2)}) %collective-permute-start.4) | collective-permute-done | bytes 786464 | tf_op jit(solution)/shard_map/ppermute | solution.py:17
  278.3 1.5 collective-permute-start.5
  279.8 0.1 constant_dynamic-update-slice_fusion.1
  279.9 9.8 %collective-permute-done.5 = bf16[128,3072]{1,0:T(8,128)(2,1)S(1)} collective-permute-done((bf16[128,3072]{1,0:T(8,128)(2,1)S(1)}, bf16[128,3072]{1,0:T(8,128)(2,1)S(1)}, u32[]{:S(2)}, u32[]{:S(2)}) %collective-permute-start.5) | collective-permute-done | bytes 786464 | tf_op jit(solution)/shard_map/ppermute | solution.py:17
  289.8 1.7 copy-done.1
  291.4 15.0 %convolution_convert_fusion.1 = bf16[512,3072]{1,0:T(8,128)(2,1)} fusion(bf16[512,3072]{1,0:T(8,128)(2,1)S(1)} %constant_dynamic-update-slice_fusion, bf16[3072,3072]{1,0:T(8,128)(2,1)} %param.6), kind=kOutput, calls=%fused_computation.2 | convolution fusion | flops 9665249280 | bytes 25165824 | tf_op jit(solution)/shard_map/dot_general | solution.py:26
  306.5 1.9 copy-done.2
  308.4 15.0 %convert_bitcast_fusion = bf16[3072,3072]{0,1:T(8,128)(2,1)} fusion(bf16[512,3072]{1,0:T(8,128)(2,1)S(1)} %copy-done.2, bf16[512,3072]{1,0:T(8,128)(2,1)} %all-gather.3.cloned.1.call-done), kind=kOutput, calls=%fused_computation | convolution fusion | flops 9673113600 | bytes 25165824 | tf_op jit(solution)/shard_map/dot_general | solution.py:26
  323.4 24.8 %copy.8 = bf16[3072,3072]{1,0:T(8,128)(2,1)} copy(bf16[3072,3072]{0,1:T(8,128)(2,1)} %convert_bitcast_fusion) | data formatting | bytes 37748736
  348.2 15.1 %convolution_convert_fusion = bf16[3072,3072]{1,0:T(8,128)(2,1)} fusion(bf16[512,3072]{1,0:T(8,128)(2,1)S(1)} %copy-done.4, bf16[512,3072]{1,0:T(8,128)(2,1)} %all-gather.5.cloned.1.call-done), kind=kOutput, calls=%fused_computation.1 | convolution fusion | flops 9673113600 | bytes 25165824 | tf_op jit(solution)/shard_map/dot_general | solution.py:26
  363.2 41.5 %reduce-scatter.11.cloned.1.call-done = bf16[64,3072]{1,0:T(8,128)(2,1)} async-done(((bf16[512,3072]{1,0:T(8,128)(2,1)}), bf16[64,3072]{1,0:T(8,128)(2,1)}) %reduce-scatter.11.cloned.1.call-update) | async-done | bytes 393232 | tf_op jit(solution)/shard_map/reduce_scatter | solution.py:42
  (28 shorter events, 0.7 us)
Async XLA Ops:
  7.2 66.2 %all-gather.3.cloned.1.call-start = ((), (), s32[]{:S(2)}) async-start(), calls=%async_computation.4 | async-start | bytes 3538944 | tf_op jit(solution)/shard_map/all_gather | solution.py:22
  7.9 118.1 %reduce-scatter.5.cloned.1.call-start = ((), (), s32[]{:S(2)}) async-start(), calls=%async_computation.5 | async-start | bytes 3932160 | tf_op jit(solution)/shard_map/reduce_scatter | solution.py:32
  89.2 99.6 %all-gather.5.cloned.1.call-start = ((), (), s32[]{:S(2)}) async-start(), calls=%async_computation.7 | async-start | bytes 3538944 | tf_op jit(solution)/shard_map/all_gather | solution.py:22
  90.0 163.1 %reduce-scatter.9.cloned.1.call-start = ((), (), s32[]{:S(2)}) async-start(), calls=%async_computation.8 | async-start | bytes 3932160 | tf_op jit(solution)/shard_map/reduce_scatter | solution.py:32
  127.6 77.2 %collective-permute-start = (bf16[128,3072]{1,0:T(8,128)(2,1)S(1)}, bf16[128,3072]{1,0:T(8,128)(2,1)S(1)}, u32[]{:S(2)}, u32[]{:S(2)}) collective-permute-start(bf16[128,3072]{1,0:T(8,128)(2,1)S(1)} %fusion.8), channel_id=1, source_target_pairs={{0,8},{8,16},{16,24},{24,0},{1,9},{9,17},{17,25},{25,1},{2,10},{10... | collective-permute-start | bytes 2359304 | tf_op jit(solution)/shard_map/ppermute | solution.py:17
  204.7 11.9 %copy-start = (bf16[128,3072]{1,0:T(8,128)(2,1)S(1)}, bf16[128,3072]{1,0:T(8,128)(2,1)}, u32[]{:S(2)}) copy-start(bf16[128,3072]{1,0:T(8,128)(2,1)} %reduce-scatter.5.cloned.1.call-done) | copy-start | bytes 2359300
  204.8 158.5 %reduce-scatter.7.cloned.1.call-start = ((), (), s32[]{:S(2)}) async-start(), calls=%async_computation.6 | async-start | bytes 3538944 | tf_op jit(solution)/shard_map/reduce_scatter | solution.py:42
  204.8 11.5 %collective-permute-start.1 = (bf16[128,3072]{1,0:T(8,128)(2,1)S(1)}, bf16[128,3072]{1,0:T(8,128)(2,1)S(1)}, u32[]{:S(2)}, u32[]{:S(2)}) collective-permute-start(bf16[128,3072]{1,0:T(8,128)(2,1)S(1)} %collective-permute-done), channel_id=1, source_target_pairs={{0,8},{8,16},{16,24},{24,0},{1,9},{9,17},{17,25},{25,1},{2,10},{10... | collective-permute-start | bytes 2359304 | tf_op jit(solution)/shard_map/ppermute | solution.py:17
  216.3 19.9 %collective-permute-start.2 = (bf16[128,3072]{1,0:T(8,128)(2,1)S(1)}, bf16[128,3072]{1,0:T(8,128)(2,1)S(1)}, u32[]{:S(2)}, u32[]{:S(2)}) collective-permute-start(bf16[128,3072]{1,0:T(8,128)(2,1)S(1)} %collective-permute-done.1), channel_id=1, source_target_pairs={{0,8},{8,16},{16,24},{24,0},{1,9},{9,17},{17,25},{25,1},{2,10},{10... | collective-permute-start | bytes 2359304 | tf_op jit(solution)/shard_map/ppermute | solution.py:17
  236.3 1.6 copy-start.3
  253.0 151.7 %reduce-scatter.11.cloned.1.call-start = ((), (), s32[]{:S(2)}) async-start(), calls=%async_computation.9 | async-start | bytes 3538944 | tf_op jit(solution)/shard_map/reduce_scatter | solution.py:42
  253.0 1.1 copy-start.5
  255.4 11.5 %collective-permute-start.3 = (bf16[128,3072]{1,0:T(8,128)(2,1)S(1)}, bf16[128,3072]{1,0:T(8,128)(2,1)S(1)}, u32[]{:S(2)}, u32[]{:S(2)}) collective-permute-start(bf16[128,3072]{1,0:T(8,128)(2,1)S(1)} %get-tuple-element.9), channel_id=1, source_target_pairs={{0,8},{8,16},{16,24},{24,0},{1,9},{9,17},{17,25},{25,1},{2,10},{10... | collective-permute-start | bytes 2359304 | tf_op jit(solution)/shard_map/ppermute | solution.py:17
  266.8 11.4 %collective-permute-start.4 = (bf16[128,3072]{1,0:T(8,128)(2,1)S(1)}, bf16[128,3072]{1,0:T(8,128)(2,1)S(1)}, u32[]{:S(2)}, u32[]{:S(2)}) collective-permute-start(bf16[128,3072]{1,0:T(8,128)(2,1)S(1)} %collective-permute-done.3), channel_id=1, source_target_pairs={{0,8},{8,16},{16,24},{24,0},{1,9},{9,17},{17,25},{25,1},{2,10},{10... | collective-permute-start | bytes 2359304 | tf_op jit(solution)/shard_map/ppermute | solution.py:17
  278.3 11.4 %collective-permute-start.5 = (bf16[128,3072]{1,0:T(8,128)(2,1)S(1)}, bf16[128,3072]{1,0:T(8,128)(2,1)S(1)}, u32[]{:S(2)}, u32[]{:S(2)}) collective-permute-start(bf16[128,3072]{1,0:T(8,128)(2,1)S(1)} %collective-permute-done.4), channel_id=1, source_target_pairs={{0,8},{8,16},{16,24},{24,0},{1,9},{9,17},{17,25},{25,1},{2,10},{10... | collective-permute-start | bytes 2359304 | tf_op jit(solution)/shard_map/ppermute | solution.py:17
  289.7 1.7 copy-start.1
  306.5 1.9 copy-start.2
  323.4 24.8 %copy-start.4 = (bf16[512,3072]{1,0:T(8,128)(2,1)S(1)}, bf16[512,3072]{1,0:T(8,128)(2,1)}, u32[]{:S(2)}) copy-start(bf16[512,3072]{1,0:T(8,128)(2,1)} %copy-done.3) | copy-start | bytes 9437188
Sparse Core Ops, SparseCore 0:
  10.2 63.1 all-gather.2
  89.4 36.5 reduce-scatter.4
  128.4 60.4 all-gather.4
  204.9 40.9 reduce-scatter.8
  253.1 74.2 reduce-scatter.6
  331.4 73.3 reduce-scatter.10
